TPU v7x, 32 devices: a whole 2x2x4 slice. The times are simulated.
32 devices in a mesh: groups: 2 (over y), head: 4 (over z), hist: 4 (over x, core).
Axes of the slice: x: 2, y: 2, z: 4, core: 2. Of those that a mesh axis runs over, the one named last changes fastest.
Arguments:
- tokens: bfloat16 [1024, 8192], P('groups', 'hist'), parts along dimension 0, may hold values from -6 to 6
- w_qkvu: bfloat16 [8192, 4, 8192], P('hist', None, 'head'), may hold values from -0.0625 to 0.0625
- k_cache: bfloat16 [4096, 8192], P(('groups', 'hist'), 'head'), parts along dimension 0, may hold values from -6 to 6
- v_cache: bfloat16 [4096, 8192], P(('groups', 'hist'), 'head'), parts along dimension 0
- w_out: bfloat16 [8192, 8192], P('head', 'hist'), may hold values from -0.0625 to 0.0625
- vis_start: int32 [1024], P('groups'), parts along dimension 0, may hold values from 0 to 511, as said below
- vis_end: int32 [1024], P('groups'), parts along dimension 0, may hold values from 1025 to 2048
Outputs:
- layer_out: bfloat16 [1024, 8192], P(('groups', 'head'), 'hist'), parts along dimension 0
There are 2 independent parts, one for each index of `groups`. A program takes and returns all parts, laid end to end along the dimension named above; an argument that names none is the same for every part. Nothing has to cross between parts.
Inputs may be any that keep to these rules, and one draw needn't show every extreme that they name: vis_start and vis_end together leave every candidate 2048 // 4 + 2 or more visible history events.
All inputs are finite; a program needn't handle non-finite values.
Results may differ from a plain program's by a relative error of at most 0.02.
Values may be sent and summed in bfloat16 or wider, within the bound.
A program may use at most 192 MiB of HBM per device.

v0:
```python
import jax
import jax.numpy as jnp
from jax import lax
from jax.sharding import PartitionSpec as P

DH = 128
epsilon = 1e-05


def history_terms(query_heads, key_block, value_block, vis_lo, vis_hi):
    head_total = query_heads.shape[1]
    head_size = query_heads.shape[2]
    block_len = key_block.shape[0]
    key_heads = key_block.reshape(block_len, head_total, head_size)
    value_heads = value_block.reshape(block_len, head_total, head_size)
    scores = jnp.einsum(
        "rhe,lhe->rhl", query_heads, key_heads, preferred_element_type=jnp.float32
    ) * head_size ** (-0.5)
    positions = lax.iota(jnp.int32, block_len)
    visible = (positions[None, :] >= vis_lo[:, None]) & (positions[None, :] < vis_hi[:, None])
    weights = jnp.where(visible[:, None, :], jax.nn.silu(scores), 0.0).astype(jnp.bfloat16)
    summed_values = jnp.einsum(
        "rhl,lhe->rhe", weights, value_heads, preferred_element_type=jnp.float32
    )
    return summed_values.reshape(query_heads.shape[0], head_total * head_size)


def local(tokens, w_qkvu, k_cache, v_cache, w_out, vis_start, vis_end):
    cand_total = tokens.shape[0]
    hist_count = lax.axis_size("hist")
    head_count = lax.axis_size("head")
    own_count = cand_total // hist_count
    own_first = lax.axis_index("hist") * own_count
    local_width = w_qkvu.shape[2]
    local_heads = local_width // DH
    full_width = local_width * head_count
    flat_weight = w_qkvu.reshape(w_qkvu.shape[0], 4 * local_width)
    start_own = lax.dynamic_slice_in_dim(vis_start, own_first, own_count)
    end_own = lax.dynamic_slice_in_dim(vis_end, own_first, own_count)
    summed = lax.psum_scatter(
        jnp.dot(tokens, flat_weight, preferred_element_type=jnp.float32).astype(jnp.bfloat16),
        "hist",
        scatter_dimension=0,
        tiled=True,
    ).astype(jnp.float32)
    own_part = jax.nn.silu(summed).astype(jnp.bfloat16).reshape(own_count, 4, local_width)
    own_query = own_part[:, 0]
    own_key = own_part[:, 1]
    own_value = own_part[:, 2]
    own_gate = own_part[:, 3]
    query_heads = own_query.reshape(own_count, local_heads, DH)
    history = history_terms(
        query_heads,
        lax.all_gather(k_cache, "hist", axis=0, tiled=True),
        lax.all_gather(v_cache, "hist", axis=0, tiled=True),
        start_own,
        end_own,
    )
    counts = (end_own - start_own).astype(jnp.float32)
    own_product = own_query.astype(jnp.float32) * own_key.astype(jnp.float32)
    own_score = jnp.sum(own_product.reshape(own_count, local_heads, DH), axis=2) * DH ** (-0.5)
    own_term = jax.nn.silu(own_score)[:, :, None] * own_value.astype(jnp.float32).reshape(
        own_count, local_heads, DH
    )
    attended = history / jnp.sqrt(counts)[:, None] + own_term.reshape(own_count, local_width)
    row_sum = lax.psum(jnp.sum(attended, axis=1), "head")
    centered = attended - (row_sum / full_width)[:, None]
    spread = lax.psum(jnp.sum(centered * centered, axis=1), "head")
    normed = centered * lax.rsqrt(spread / full_width + epsilon)[:, None]
    gated_rows = (normed * own_gate.astype(jnp.float32)).astype(jnp.bfloat16)
    gathered = lax.all_gather(gated_rows, "hist", axis=0, tiled=True)
    out_count = cand_total // head_count
    out_first = lax.axis_index("head") * out_count
    whole_out = jnp.dot(gathered, w_out, preferred_element_type=jnp.float32)
    total_out = lax.psum(whole_out.astype(jnp.bfloat16), "head").astype(jnp.float32)
    summed_out = lax.dynamic_slice_in_dim(total_out, out_first, out_count, 0)
    residual = lax.dynamic_slice_in_dim(tokens, out_first, out_count, 0).astype(jnp.float32)
    return (residual + summed_out).astype(jnp.bfloat16)


def solution(mesh):
    in_specs = (
        P("groups", "hist"),
        P("hist", None, "head"),
        P(("groups", "hist"), "head"),
        P(("groups", "hist"), "head"),
        P("head", "hist"),
        P("groups"),
        P("groups"),
    )
    out_specs = P(("groups", "head"), "hist")
    return jax.shard_map(local, mesh=mesh, in_specs=in_specs, out_specs=out_specs, check_vma=False)
```

profile of v0, /device:TPU:0, one launch (start us, length us, event | category | flops | bytes accessed | tf_op | source)
XLA Modules:
  0.0 367.3 jit_solution(18409414456210205719)
XLA Ops:
  6.5 0.0 all-gather.6.cloned.1.call-start
  6.5 0.7 all-gather.6.cloned.1.call-update
  7.3 0.0 reduce-scatter.2.cloned.1.call-start
  7.3 0.0 copy-start.2
  7.3 30.2 %copy.29 = bf16[256,8,4,2048]{3,1,2,0:T(8,128)(2,1)} copy(bf16[256,8,4,2048]{3,2,1,0:T(4,128)(2,1)} %bitcast.58) | data formatting | bytes 67108864
  37.5 0.0 copy-done.2
  37.5 25.5 %convolution_convert_fusion = bf16[512,8192]{1,0:T(8,128)(2,1)} fusion(bf16[512,2048]{1,0:T(8,128)(2,1)S(1)} %copy-done.2, bf16[2048,8192]{1,0:T(8,128)(2,1)} %bitcast.59), kind=kOutput, calls=%fused_computation.7 | convolution fusion | flops 17184063488 | bytes 44040192 | tf_op jit(solution)/shard_map/dot_general | solution.py:41
  63.0 0.0 copy-start.1
  63.0 0.0 reduce-scatter.2.cloned.1.call-update
  63.0 0.0 all-gather.4.cloned.1.call-start
  63.1 1.6 copy-done.1
  64.7 2.5 copy.14
  67.2 0.0 all-gather.4.cloned.1.call-update
  67.3 0.2 all-gather.8.cloned.1.call-start
  67.5 0.8 convert_sqrt_fusion
  68.3 0.5 fusion.19
  68.8 1.1 all-gather.6.cloned.1.call-done
  69.9 12.4 %copy.17 = bf16[2048,2048]{0,1:T(8,128)(2,1)} copy(bf16[2048,2048]{1,0:T(8,128)(2,1)} %all-gather.6.cloned.1.call-done) | data formatting | bytes 16777216 | tf_op jit(solution)/shard_map/all_gather | solution.py:55
  82.3 61.6 %reduce-scatter.2.cloned.1.call-done = bf16[128,8192]{1,0:T(8,128)(2,1)} async-done(((bf16[512,8192]{1,0:T(8,128)(2,1)}), bf16[128,8192]{1,0:T(8,128)(2,1)}) %reduce-scatter.2.cloned.1.call-update) | async-done | bytes 2097168 | tf_op jit(solution)/shard_map/reduce_scatter | solution.py:40
  143.9 4.0 %fusion.12 = bf16[128,8192]{1,0:T(8,128)(2,1)} fusion(bf16[128,8192]{1,0:T(8,128)(2,1)} %reduce-scatter.2.cloned.1.call-done), kind=kLoop, calls=%fused_computation.15 | loop fusion | flops 6291456 | bytes 4194304 | tf_op jit(solution)/shard_map/convert_element_type | solution.py:46
  148.0 3.3 reshape.92
  151.3 4.4 %fusion.24 = (bf16[128,1,2048]{2,1,0:T(2,128)(2,1)S(1)}, bf16[128,1,2048]{2,1,0:T(2,128)(2,1)}, f32[128,1,2048]{2,1,0:T(1,128)}, bf16[128,1,2048]{2,1,0:T(2,128)(2,1)}) fusion(bf16[128,4,2048]{2,1,0:T(4,128)(2,1)S(1)} %reshape.92), kind=kLoop, calls=%fused_computation.42 | loop fusion | flops 262144 | bytes 4718592 | tf_op jit(solution)/shard_map/slice | solution.py:49
  155.7 2.5 copy.27
  158.2 2.4 copy.26
  160.6 0.0 copy-start
  160.7 0.2 fusion.14
  160.8 0.6 copy-done
  161.5 0.1 mul.90
  161.5 1.3 copy.21
  162.9 0.4 copy_convert_fusion
  163.2 0.3 copy.22
  163.6 40.2 %all-gather.4.cloned.1.call-done = bf16[2048,2048]{0,1:T(8,128)(2,1)} async-done(((bf16[512,2048]{0,1:T(8,128)(2,1)}), bf16[2048,2048]{0,1:T(8,128)(2,1)}) %all-gather.4.cloned.1.call-update) | async-done | bytes 8388624 | tf_op jit(solution)/shard_map/all_gather | solution.py:54
  203.8 11.9 %fusion.23 = (f32[128]{0:T(128)S(1)}, f32[16,128,128]{1,2,0:T(8,128)S(1)}) fusion(f32[128,16,128]{0,2,1:T(8,128)S(1)} %bitcast.61, f32[128,16]{0,1:T(8,128)S(1)} %divide_multiply_fusion, f32[128]{0:T(128)S(1)} %get-tuple-element.5, bf16[2048,16,128]{0,2,1:T(8,128)(2,1)} %bitcast.60, pred[128,2048]{1,0:T(8,128)(4,1)S(1)} %fusion.19, ...), kind=kOutput, calls=%fused_computation.41 | convolution fusion | flops 2177892352 | bytes 19670016 | tf_op jit(solution)/shard_map/rhl,lhe->rhe/dot_general | solution.py:22
  215.7 1.3 copy.18
  217.1 11.6 %psum.21 = f32[128]{0:T(128)S(1)} all-reduce(f32[128]{0:T(128)S(1)} %get-tuple-element.12), channel_id=1, replica_groups=mesh['groups'=2,'head'=4,'hist'=4] {'head'}, use_global_device_ids=true, to_apply=%region_3.4 | all-reduce | flops 128 | bytes 1024 | tf_op jit(solution)/shard_map/psum | solution.py:66
  228.7 0.3 multiply_reduce_fusion
  229.0 8.4 %psum.22 = f32[128]{0:T(128)S(1)} all-reduce(f32[128]{0:T(128)S(1)} %multiply_reduce_fusion), channel_id=1, replica_groups=mesh['groups'=2,'head'=4,'hist'=4] {'head'}, use_global_device_ids=true, to_apply=%region_5.6 | all-reduce | flops 128 | bytes 1024 | tf_op jit(solution)/shard_map/psum | solution.py:68
  237.4 3.7 %fusion.13 = bf16[128,2048]{1,0:T(8,128)(2,1)} fusion(f32[128,1,2048]{2,1,0:T(1,128)} %get-tuple-element.10, f32[128,2048]{1,0:T(8,128)} %copy.21, f32[128,2048]{1,0:T(8,128)} %copy.18, f32[128]{0:T(128)S(1)} %add_rsqrt_fusion, f32[128]{0:T(128)S(1)} %broadcast_multiply_fusion, f32[128]{0:T(128)S(1)} %get-tuple-element.5, ...), kind=kLoop, calls=%fused_computation.19 | loop fusion | flops 2097152 | bytes 4195840 | tf_op jit(solution)/shard_map/convert_element_type | solution.py:70
  241.1 0.0 all-gather.8.cloned.1.call-update
  241.1 0.3 all-reduce.2.cloned.1.call-start
  241.4 21.1 %all-gather.8.cloned.1.call-done = bf16[512,2048]{1,0:T(8,128)(2,1)} async-done(((bf16[128,2048]{1,0:T(8,128)(2,1)}), bf16[512,2048]{1,0:T(8,128)(2,1)}) %all-gather.8.cloned.1.call-update) | async-done | bytes 2097168 | tf_op jit(solution)/shard_map/all_gather | solution.py:71
  262.5 9.9 %convolution_convert_fusion.1 = bf16[512,2048]{1,0:T(8,128)(2,1)} fusion(bf16[512,2048]{1,0:T(8,128)(2,1)} %all-gather.8.cloned.1.call-done, bf16[2048,2048]{1,0:T(8,128)(2,1)} %param.11), kind=kOutput, calls=%fused_computation.16 | convolution fusion | flops 4296015872 | bytes 12582912 | tf_op jit(solution)/shard_map/dot_general | solution.py:74
  272.4 0.0 all-reduce.2.cloned.1.call-update
  272.4 86.3 %all-reduce.2.cloned.1.call-done = bf16[512,2048]{1,0:T(8,128)(2,1)} async-done(((bf16[512,2048]{1,0:T(8,128)(2,1)}), bf16[512,2048]{1,0:T(8,128)(2,1)}) %all-reduce.2.cloned.1.call-update) | async-done | bytes 2097168 | tf_op jit(solution)/shard_map/psum | solution.py:75
  358.7 2.1 add_convert_fusion
  (3 shorter events, 0.0 us)
Async XLA Ops:
  6.5 63.4 %all-gather.6.cloned.1.call-start = ((), (), s32[]{:S(2)}) async-start(), calls=%async_computation.3 | async-start | bytes 10485760 | tf_op jit(solution)/shard_map/all_gather | solution.py:55
  7.3 136.7 %reduce-scatter.2.cloned.1.call-start = ((), (), s32[]{:S(2)}) async-start(), calls=%async_computation.1 | async-start | bytes 10485760 | tf_op jit(solution)/shard_map/reduce_scatter | solution.py:40
  7.3 30.2 %copy-start.2 = (bf16[512,2048]{1,0:T(8,128)(2,1)S(1)}, bf16[512,2048]{1,0:T(8,128)(2,1)}, u32[]{:S(2)}) copy-start(bf16[512,2048]{1,0:T(8,128)(2,1)} %param.7) | copy-start | bytes 6291460
  63.0 1.7 copy-start.1
  63.0 140.8 %all-gather.4.cloned.1.call-start = ((), (), s32[]{:S(2)}) async-start(), calls=%async_computation.2 | async-start | bytes 10485760 | tf_op jit(solution)/shard_map/all_gather | solution.py:54
  67.3 195.3 %all-gather.8.cloned.1.call-start = ((), (), s32[]{:S(2)}) async-start(), calls=%async_computation.4 | async-start | bytes 2621440 | tf_op jit(solution)/shard_map/all_gather | solution.py:71
  160.6 0.8 copy-start
  241.1 117.6 %all-reduce.2.cloned.1.call-start = ((), (), s32[]{:S(2)}) async-start(), calls=%async_computation.5 | async-start | bytes 4194304 | tf_op jit(solution)/shard_map/psum | solution.py:75
Sparse Core Ops, SparseCore 0:
  8.9 60.9 all-gather.5
  72.5 71.4 reduce-scatter.1
  145.5 58.2 all-gather.3
  241.3 21.2 all-gather.7
  272.5 86.1 all-reduce.1
where the time goes:
time: 368 us; the launch traced here: 367 us
  waiting for transfers between devices  211 us (57%)
  local copies, waits for them, and re-layouts  58.7 us (16%)
  matrix products  47.3 us (13%)
  blocking collectives  20 us (5%)
  other arithmetic  16.3 us (4%)
  between operations  13.2 us (4%)
    psum x1, waiting for transfers between devices, local(): lax.psum(whole_out.astype(jnp.bfloat16), 'head').astype(jnp.float32)  86.3 us
    reduce_scatter x1, waiting for transfers between devices, local(): lax.psum_scatter(jnp.dot(tokens, flat_weight, preferred_element_type=jnp....  61.6 us
    all_gather x1, waiting for transfers between devices, local(): lax.all_gather(k_cache, 'hist', axis=0, tiled=True)  40.2 us
    unnamed x10, local copies, waits for them, and re-layouts  39.9 us
    dot_general x1, matrix products, local(): jnp.dot(tokens, flat_weight, preferred_element_type=jnp.float32)  25.5 us
    all_gather x1, waiting for transfers between devices, local(): gathered = lax.all_gather(gated_rows, 'hist', axis=0, tiled=True)  21.1 us
    all_gather x1, local copies, waits for them, and re-layouts, local(): lax.all_gather(v_cache, 'hist', axis=0, tiled=True)  12.4 us
    dot_general x1, matrix products, history_terms(): jnp.einsum('rhl,lhe->rhe', weights, value_heads, preferred_element_type=j...  11.9 us
  transfers between devices with their start and end apart: 5, of which 5 were waited for; matrix products, arithmetic and copies ran while one was open for 25% of the time, Pallas kernels for 0%

commit v1 on v0

--- a/solution.py
+++ b/solution.py
@@ -2,9 +2,24 @@
 import jax.numpy as jnp
 from jax import lax
 from jax.sharding import PartitionSpec as P
+from jax.lax import axis_index, axis_size, ppermute
 
 DH = 128
 epsilon = 1e-05
+
+
+def bench_refer(piece_in):
+    outcome_arr = axis_size("hist")
+    value_now, a_now, p_next = (outcome_arr, axis_index("hist"), piece_in.shape[0])
+    clean, right_arr = (piece_in, 1)
+    while right_arr < value_now:
+        found = []
+        for j in range(value_now):
+            found.append((j, (j - right_arr) % value_now))
+        current_value = ppermute(clean, "hist", found)
+        clean = jnp.concatenate([clean, current_value], 0)
+        right_arr = 2 * right_arr
+    return jnp.roll(clean, a_now * p_next, 0)
 
 
 def history_terms(query_heads, key_block, value_block, vis_lo, vis_hi):
@@ -51,7 +66,7 @@
     query_heads = own_query.reshape(own_count, local_heads, DH)
     history = history_terms(
         query_heads,
-        lax.all_gather(k_cache, "hist", axis=0, tiled=True),
+        bench_refer(k_cache),
         lax.all_gather(v_cache, "hist", axis=0, tiled=True),
         start_own,
         end_own,

time: 368 us -> 448 us (1.22)
  waiting for transfers between devices: 211 us -> 262 us
  local copies, waits for them, and re-layouts: 58.7 us -> 82.9 us
    ppermute x0 -> x2, waiting for transfers between devices: none -> 154 us  [bench_refer(): current_value = ppermute(clean, 'hist', found)]
    reduce_scatter x1, waiting for transfers between devices: 61.6 us -> 0.01 us  [local(): lax.psum_scatter(jnp.dot(tokens, flat_weight, preferred_element_type=jnp....]
    all_gather x1 -> x0, waiting for transfers between devices: 40.2 us -> none  [local(): lax.all_gather(k_cache, 'hist', axis=0, tiled=True)]
    unnamed x10 -> x17, local copies, waits for them, and re-layouts: 39.9 us -> 52.1 us
    dynamic_slice x0 -> x1, local copies, waits for them, and re-layouts: none -> 8.38 us  [bench_refer(): return jnp.roll(clean, a_now * p_next, 0)]
    concatenate x0 -> x1, local copies, waits for them, and re-layouts: none -> 4.71 us  [bench_refer(): return jnp.roll(clean, a_now * p_next, 0)]
  transfers between devices with their start and end apart: 5 -> 6, of which waited for: 5 -> 4; matrix products, arithmetic and copies ran while one was open for 25% -> 22% of each run, Pallas kernels for 0% -> 0%
where the time goes in v1:
time: 448 us; the launch traced here: 447 us
  waiting for transfers between devices  262 us (58%)
  local copies, waits for them, and re-layouts  82.9 us (19%)
  matrix products  47.6 us (11%)
  blocking collectives  20 us (4%)
  other arithmetic  18.5 us (4%)
  between operations  13.3 us (3%)
    ppermute x2, waiting for transfers between devices, bench_refer(): current_value = ppermute(clean, 'hist', found)  154 us
    psum x1, waiting for transfers between devices, local(): lax.psum(whole_out.astype(jnp.bfloat16), 'head').astype(jnp.float32)  86.3 us
    unnamed x17, local copies, waits for them, and re-layouts  52.1 us
    dot_general x1, matrix products, local(): jnp.dot(tokens, flat_weight, preferred_element_type=jnp.float32)  25.5 us
    all_gather x1, waiting for transfers between devices, local(): gathered = lax.all_gather(gated_rows, 'hist', axis=0, tiled=True)  21.1 us
    all_gather x1, local copies, waits for them, and re-layouts, local(): lax.all_gather(v_cache, 'hist', axis=0, tiled=True)  12.3 us
    dot_general x1, matrix products, history_terms(): jnp.einsum('rhl,lhe->rhe', weights, value_heads, preferred_element_type=j...  12.2 us
    psum x1, blocking collectives, local(): row_sum = lax.psum(jnp.sum(attended, axis=1), 'head')  11.7 us
  transfers between devices with their start and end apart: 6, of which 4 were waited for; matrix products, arithmetic and copies ran while one was open for 22% of the time, Pallas kernels for 0%

profile of v1, /device:TPU:0, one launch (start us, length us, event | category | flops | bytes accessed | tf_op | source)
XLA Modules:
  0.0 447.2 jit_solution(1965757129780877837)
XLA Ops:
  6.5 0.0 all-gather.3.cloned.1.call-start
  6.5 0.7 all-gather.3.cloned.1.call-update
  7.3 0.0 reduce-scatter.2.cloned.1.call-start
  7.3 0.0 copy-start.3
  7.3 30.2 %copy.35 = bf16[256,8,4,2048]{3,1,2,0:T(8,128)(2,1)} copy(bf16[256,8,4,2048]{3,2,1,0:T(4,128)(2,1)} %bitcast.58) | data formatting | bytes 67108864
  37.5 0.0 copy-done.3
  37.5 25.5 %convolution_convert_fusion = bf16[512,8192]{1,0:T(8,128)(2,1)} fusion(bf16[512,2048]{1,0:T(8,128)(2,1)S(1)} %copy-done.3, bf16[2048,8192]{1,0:T(8,128)(2,1)} %bitcast.59), kind=kOutput, calls=%fused_computation.7 | convolution fusion | flops 17184063488 | bytes 44040192 | tf_op jit(solution)/shard_map/dot_general | solution.py:56
  63.1 0.0 reduce-scatter.2.cloned.1.call-update
  63.1 0.0 all-gather.5.cloned.1.call-start
  63.1 2.9 copy.16
  66.1 2.4 collective-permute-start
  68.5 23.6 %collective-permute-done = bf16[512,2048]{0,1:T(8,128)(2,1)S(1)} collective-permute-done((bf16[512,2048]{0,1:T(8,128)(2,1)S(1)}, bf16[512,2048]{0,1:T(8,128)(2,1)S(1)}, u32[]{:S(2)}, u32[]{:S(2)}) %collective-permute-start) | collective-permute-done | bytes 2097184 | tf_op jit(solution)/shard_map/ppermute | solution.py:19
  92.0 0.0 copy-start
  92.0 1.3 copy-done
  93.3 2.7 pad_maximum_fusion
  96.1 0.4 collective-permute-start.1
  96.5 0.8 convert_sqrt_fusion
  97.2 1.6 constant_dynamic-update-slice_fusion.5
  98.8 0.2 fusion.19
  99.0 0.0 copy-start.1
  99.1 3.3 constant_dynamic-update-slice_fusion.4
  102.4 130.0 %collective-permute-done.1 = bf16[1024,2048]{0,1:T(8,128)(2,1)} collective-permute-done((bf16[1024,2048]{0,1:T(8,128)(2,1)}, bf16[1024,2048]{0,1:T(8,128)(2,1)}, u32[]{:S(2)}, u32[]{:S(2)}) %collective-permute-start.1) | collective-permute-done | bytes 4194336 | tf_op jit(solution)/shard_map/ppermute | solution.py:19
  232.4 4.6 %constant_dynamic-update-slice_fusion.3 = bf16[4096,2048]{0,1:T(8,128)(2,1)} fusion(bf16[4096,2048]{0,1:T(8,128)(2,1)} %constant_dynamic-update-slice_fusion.4, bf16[1024,2048]{0,1:T(8,128)(2,1)} %collective-permute-done.1), kind=kLoop, calls=%fused_computation.38 | loop fusion | bytes 8388608
  237.0 1.6 constant_dynamic-update-slice_fusion.2
  238.6 0.0 copy-done.1
  238.6 1.6 constant_dynamic-update-slice_fusion.1
  240.2 4.7 %constant_dynamic-update-slice_fusion = bf16[4096,2048]{0,1:T(8,128)(2,1)} fusion(bf16[4096,2048]{0,1:T(8,128)(2,1)} %constant_dynamic-update-slice_fusion.1, bf16[1024,2048]{0,1:T(8,128)(2,1)} %collective-permute-done.1), kind=kLoop, calls=%fused_computation.35 | loop fusion | bytes 8388608 | tf_op jit(solution)/shard_map/jit(_roll_dynamic)/concatenate | solution.py:22
  244.9 8.4 %constant_dynamic-slice_fusion = bf16[2048,2048]{0,1:T(8,128)(2,1)} fusion(bf16[4096,2048]{0,1:T(8,128)(2,1)} %constant_dynamic-update-slice_fusion, s32[]{:T(128)S(6)} %select_n.28), kind=kLoop, calls=%fused_computation.42 | loop fusion | bytes 16777220 | tf_op jit(solution)/shard_map/jit(_roll_dynamic)/dynamic_slice | solution.py:22
  253.3 0.0 all-gather.3.cloned.1.call-done
  253.3 12.3 %copy.21 = bf16[2048,2048]{0,1:T(8,128)(2,1)} copy(bf16[2048,2048]{1,0:T(8,128)(2,1)} %all-gather.3.cloned.1.call-done) | data formatting | bytes 16777216 | tf_op jit(solution)/shard_map/all_gather | solution.py:70
  265.6 0.0 reduce-scatter.2.cloned.1.call-done
  265.6 4.0 fusion.12
  269.7 3.3 reshape.93
  273.0 4.4 fusion.24
  277.4 2.4 copy.32
  279.8 0.0 copy-start.2
  279.8 2.6 copy.33
  282.4 0.2 fusion.14
  282.6 0.0 copy-done.2
  282.6 0.4 copy_convert_fusion
  283.0 0.3 copy.27
  283.3 12.2 %fusion.23 = (f32[128]{0:T(128)S(1)}, f32[16,128,128]{1,2,0:T(8,128)S(1)}) fusion(f32[128,16,128]{0,2,1:T(8,128)S(1)} %bitcast.63, f32[128,16]{0,1:T(8,128)S(1)} %divide_multiply_fusion, f32[128]{0:T(128)S(1)} %get-tuple-element.5, bf16[2048,16,128]{0,2,1:T(8,128)(2,1)} %bitcast.61, pred[128,2048]{0,1:T(8,128)(4,1)S(1)} %fusion.19, ...), kind=kOutput, calls=%fused_computation.49 | convolution fusion | flops 2177892352 | bytes 19670016 | tf_op jit(solution)/shard_map/rhl,lhe->rhe/dot_general | solution.py:37
  295.5 11.7 %psum.21 = f32[128]{0:T(128)S(1)} all-reduce(f32[128]{0:T(128)S(1)} %get-tuple-element.12), channel_id=1, replica_groups=mesh['groups'=2,'head'=4,'hist'=4] {'head'}, use_global_device_ids=true, to_apply=%region_3.4 | all-reduce | flops 128 | bytes 1024 | tf_op jit(solution)/shard_map/psum | solution.py:81
  307.1 0.3 multiply_reduce_fusion
  307.5 8.4 %psum.22 = f32[128]{0:T(128)S(1)} all-reduce(f32[128]{0:T(128)S(1)} %multiply_reduce_fusion), channel_id=1, replica_groups=mesh['groups'=2,'head'=4,'hist'=4] {'head'}, use_global_device_ids=true, to_apply=%region_5.6 | all-reduce | flops 128 | bytes 1024 | tf_op jit(solution)/shard_map/psum | solution.py:83
  315.8 0.3 copy.23
  316.2 0.1 mul.94
  316.2 1.3 copy.26
  317.6 3.4 fusion.13
  320.9 0.0 all-gather.5.cloned.1.call-update
  321.0 0.3 all-reduce.2.cloned.1.call-start
  321.2 21.1 %all-gather.5.cloned.1.call-done = bf16[512,2048]{1,0:T(8,128)(2,1)} async-done(((bf16[128,2048]{1,0:T(8,128)(2,1)}), bf16[512,2048]{1,0:T(8,128)(2,1)}) %all-gather.5.cloned.1.call-update) | async-done | bytes 2097168 | tf_op jit(solution)/shard_map/all_gather | solution.py:86
  342.4 9.9 %convolution_convert_fusion.1 = bf16[512,2048]{1,0:T(8,128)(2,1)} fusion(bf16[512,2048]{1,0:T(8,128)(2,1)} %all-gather.5.cloned.1.call-done, bf16[2048,2048]{1,0:T(8,128)(2,1)} %param.11), kind=kOutput, calls=%fused_computation.17 | convolution fusion | flops 4296015872 | bytes 12582912 | tf_op jit(solution)/shard_map/dot_general | solution.py:89
  352.2 0.0 all-reduce.2.cloned.1.call-update
  352.3 86.3 %all-reduce.2.cloned.1.call-done = bf16[512,2048]{1,0:T(8,128)(2,1)} async-done(((bf16[512,2048]{1,0:T(8,128)(2,1)}), bf16[512,2048]{1,0:T(8,128)(2,1)}) %all-reduce.2.cloned.1.call-update) | async-done | bytes 2097168 | tf_op jit(solution)/shard_map/psum | solution.py:90
  438.6 2.1 add_convert_fusion
  (3 shorter events, 0.0 us)
Async XLA Ops:
  6.5 246.8 %all-gather.3.cloned.1.call-start = ((), (), s32[]{:S(2)}) async-start(), calls=%async_computation.2 | async-start | bytes 10485760 | tf_op jit(solution)/shard_map/all_gather | solution.py:70
  7.3 258.4 %reduce-scatter.2.cloned.1.call-start = ((), (), s32[]{:S(2)}) async-start(), calls=%async_computation.1 | async-start | bytes 10485760 | tf_op jit(solution)/shard_map/reduce_scatter | solution.py:55
  7.3 30.2 %copy-start.3 = (bf16[512,2048]{1,0:T(8,128)(2,1)S(1)}, bf16[512,2048]{1,0:T(8,128)(2,1)}, u32[]{:S(2)}) copy-start(bf16[512,2048]{1,0:T(8,128)(2,1)} %param.7) | copy-start | bytes 6291460
  63.1 279.3 %all-gather.5.cloned.1.call-start = ((), (), s32[]{:S(2)}) async-start(), calls=%async_computation.3 | async-start | bytes 2621440 | tf_op jit(solution)/shard_map/all_gather | solution.py:86
  66.1 26.0 %collective-permute-start = (bf16[512,2048]{0,1:T(8,128)(2,1)S(1)}, bf16[512,2048]{0,1:T(8,128)(2,1)S(1)}, u32[]{:S(2)}, u32[]{:S(2)}) collective-permute-start(bf16[512,2048]{0,1:T(8,128)(2,1)S(1)} %copy.16), channel_id=1, source_target_pairs={{0,3},{1,0},{2,1},{3,2},{4,7},{5,4},{6,5},{7,6},{8,11},{9,8},{10,9... | collective-permute-start | bytes 6291464 | tf_op jit(solution)/shard_map/ppermute | solution.py:19
  92.0 1.3 copy-start
  96.1 136.3 %collective-permute-start.1 = (bf16[1024,2048]{0,1:T(8,128)(2,1)}, bf16[1024,2048]{0,1:T(8,128)(2,1)}, u32[]{:S(2)}, u32[]{:S(2)}) collective-permute-start(bf16[1024,2048]{0,1:T(8,128)(2,1)} %pad_maximum_fusion), channel_id=1, source_target_pairs={{0,2},{1,3},{2,0},{3,1},{4,6},{5,7},{6,4},{7,5},{8,10},{9,11},{10,... | collective-permute-start | bytes 12582920 | tf_op jit(solution)/shard_map/ppermute | solution.py:19
  99.0 139.6 %copy-start.1 = (bf16[512,2048]{0,1:T(8,128)(2,1)S(1)}, bf16[512,2048]{0,1:T(8,128)(2,1)}, u32[]{:S(2)}) copy-start(bf16[512,2048]{0,1:T(8,128)(2,1)} %copy-done) | copy-start | bytes 6291460
  279.8 2.8 copy-start.2
  321.0 117.6 %all-reduce.2.cloned.1.call-start = ((), (), s32[]{:S(2)}) async-start(), calls=%async_computation.4 | async-start | bytes 4194304 | tf_op jit(solution)/shard_map/psum | solution.py:90
Sparse Core Ops, SparseCore 0:
  8.9 60.9 all-gather.2
  72.5 114.3 reduce-scatter.1
  321.1 21.2 all-gather.4
  352.4 86.1 all-reduce.1
